TPU v7x, 32 devices: a whole 2x2x4 slice. The times are simulated.
32 devices in a mesh: walk: 4 (over x, core), pb: 8 (over z, y).
Axes of the slice: x: 2, y: 2, z: 4, core: 2. Of those that a mesh axis runs over, the one named last changes fastest.
Arguments:
- greens: bfloat16 [64, 64, 3072], P('walk', 'pb'), may hold values from -6 to 6
- cholesky: bfloat16 [32, 300, 3072], P('pb'), may hold values from -0.011962891 to 0.011962891
- slot_source: int32 [32], replicated, may hold values from 0 to 63, as said below
- block_transfer_index: int32 [32], P('pb'), may hold values from 0 to 15
- slot_multiplicity: int32 [32], P('pb'), may hold values from 0 to 3, as said below
- fields: float32 [64, 16, 300], P('walk'), may hold values from -6 to 6
- weight: float32 [64], P('walk'), may hold values from 0.2 to 5
Outputs:
- force_bias: float32 [64, 2, 4800], P('walk', None, 'pb')
- local_energy: float32 [64], P('walk')
- new_weight: float32 [64], P('walk')
- mixed_energy: float32 [], replicated
Inputs may be any that keep to these rules, and one draw needn't show every extreme that they name: `slot_source`: the Green's block of k-point k lies on index k // 8 of pb; with P = 8, slot j of pb index d (slot d * 4 + j) reads a block that lies on index (d + o_j) mod P of pb, where o_0 = 0, o_1 = P - 1, o_2 = 1, o_3 = P // 2. `slot_multiplicity`: 0 marks an empty slot; on each index of pb the live slots come first, and on some index all 4 slots are live.
All inputs are finite; a program needn't handle non-finite values.
Results may differ from a plain program's by a relative error of at most 0.0003.
Values may be sent and summed in bfloat16 or wider, within the bound.
A program may use at most 320 MiB of HBM per device.

v0:
```python
import functools

import jax
import jax.numpy as jnp
import numpy as np
from jax import lax
from jax.experimental import pallas as pl
from jax.experimental.pallas import tpu as pltpu
from jax.sharding import PartitionSpec as P

ORBITAL_COUNT = 96
OCCUPIED_COUNT = 16
TRANSFER_COUNT = 16
SQRT_STEP = 0.05

DOUBLED = 2 * ORBITAL_COUNT
PAIR = 2 * DOUBLED
WINDOW = 256
SHIFT = PAIR - WINDOW
LANES = 128
VMEM_LIMIT = 60 * 1024 * 1024
F32 = jnp.float32


def offsets_of(devices):
    return [0, devices - 1, 1, devices // 2]


def arrangement():
    table = np.zeros((2, WINDOW, 2, 2, WINDOW), np.float32)
    for parity in range(2):
        start = parity * (DOUBLED - SHIFT)
        for window in range(2):
            out = window * (DOUBLED - SHIFT)
            for q in range(ORBITAL_COUNT):
                re, im = start + q, start + ORBITAL_COUNT + q
                first, second = out + q, out + ORBITAL_COUNT + q
                table[parity, re, window, 0, first] = 1.0
                table[parity, im, window, 0, second] = -1.0
                table[parity, im, window, 1, first] = 1.0
                table[parity, re, window, 1, second] = 1.0
    return table.reshape(2, WINDOW, 4 * WINDOW)


def select_kernel(devices, source_ref, greens_ref, *rest):
    me = lax.axis_index("pb")
    walkers, kpoints, _ = greens_ref.shape
    outs, (wide, picked) = rest[:-2], rest[-2:]
    slots = len(outs)
    for w in range(walkers):
        wide[w] = greens_ref[w].astype(F32)
    for slot in range(slots):
        requester = lax.rem(me + devices - offsets_of(devices)[slot], devices)
        index = lax.rem(source_ref[requester * slots + slot], kpoints)
        for w in range(walkers):
            picked[slot, w : w + 1, :] = wide[w, pl.ds(index, 1), :]
        outs[slot][...] = picked[slot].astype(greens_ref.dtype)


def row_of(part, occupied, walkers):
    half = (OCCUPIED_COUNT // 2) * walkers
    return part * 2 * half + (occupied % 2) * half + (occupied // 2) * walkers


def compute_kernel(
    transfer_ref, multiple_ref, chol_ref, table_ref, *rest
):
    greens, (dense_ref, cross_ref, operand, product, diagonal, crossed, green, tails) = rest[:-8], rest[-8:]
    slot = pl.program_id(0)
    slots = pl.num_programs(0)
    walkers = green.shape[0]
    vectors = chol_ref.shape[1]
    half = (OCCUPIED_COUNT // 2) * walkers
    pairs = OCCUPIED_COUNT // 2
    scaled = multiple_ref[slot].astype(F32)

    for index, green_ref in enumerate(greens):

        @pl.when(slot == index)
        def _():
            green[...] = green_ref[...]


    for parity in range(2):
        rows = jnp.concatenate(
            [green[:, PAIR * p + SHIFT * parity : PAIR * p + SHIFT * parity + WINDOW] for p in range(pairs)], 0
        )
        spread = jnp.dot(rows, table_ref[parity], preferred_element_type=F32).astype(operand.dtype)
        for window in range(2):
            for part in range(2):
                at = (window * 2 + part) * WINDOW
                operand[window, pl.ds(part * 2 * half + parity * half, half), :] = spread[:, at : at + WINDOW]

    main = vectors // WINDOW * WINDOW
    rest_count = vectors - main

    @pl.when(slot == 0)
    def _():
        tails[...] = jnp.zeros_like(tails)

    def window_of(i):
        start = PAIR * (i // 2) + SHIFT * (i % 2)
        return slice(start, start + WINDOW)

    def times(parity, right):
        return lax.dot_general(operand[parity], right, (((1,), (1,)), ((), ())), preferred_element_type=F32)

    for i in range(OCCUPIED_COUNT):
        tails[i % 2, pl.ds(LANES * (i // 2), rest_count), :] = chol_ref[0, main:vectors, window_of(i)]
    for parity in range(2):
        ends = times(parity, tails[parity])
        for p in range(pairs):
            product[2 * p + parity, :, main : main + LANES] = ends[:, LANES * p : LANES * (p + 1)]

    def multiply(i):
        product[i, :, :main] = times(i % 2, chol_ref[0, :main, window_of(i)])

    def block(i, j, part):
        return product[i, pl.ds(row_of(part, j, walkers), walkers), :]

    zero = jnp.zeros((walkers, main + LANES), F32)
    off = [zero, zero]
    own = [zero, zero]
    trace = [zero, zero]
    multiply(0)
    for i in range(OCCUPIED_COUNT):
        if i + 1 < OCCUPIED_COUNT:
            multiply(i + 1)
        for part in range(2):
            here = block(i, i, part)
            own[part] = own[part] + here * here
            trace[part] = trace[part] + here
            for j in range(i):
                off[part] = off[part] + block(i, j, part) * block(j, i, part)
    for part in range(2):
        diagonal[slot, part] = scaled * trace[part][:, :vectors]
    total = scaled * ((own[0] - own[1]) + 2.0 * (off[0] - off[1]))[:, :vectors]

    @pl.when(slot == 0)
    def _():
        crossed[...] = total

    @pl.when(slot > 0)
    def _():
        crossed[...] += total

    @pl.when(slot == slots - 1)
    def _():
        held = diagonal.shape[0]
        cross_ref[...] = jnp.sum(crossed[...], axis=1, keepdims=True)
        shares, _, _, width = dense_ref.shape
        for t in range(TRANSFER_COUNT):
            keep = [(transfer_ref[s] == t).astype(jnp.int32).astype(F32) for s in range(held)]
            for part in range(2):
                value = keep[0] * diagonal[0, part]
                for s in range(1, held):
                    value = value + keep[s] * diagonal[s, part]
                low, high = t * vectors, (t + 1) * vectors
                for share in range(low // width, (high - 1) // width + 1):
                    first, last = max(low, share * width), min(high, (share + 1) * width)
                    dense_ref[share, part, :, first - share * width : last - share * width] = value[
                        :, first - low : last - low
                    ]


def on_diagonal(count):
    return lax.broadcasted_iota(jnp.int32, (count, count), 0) == lax.broadcasted_iota(jnp.int32, (count, count), 1)


def column_of(row):
    count = row.shape[1]
    return jnp.sum(jnp.where(on_diagonal(count), jnp.broadcast_to(row, (count, count)), 0.0), axis=1, keepdims=True)


def row_from(column):
    count = column.shape[0]
    return jnp.sum(jnp.where(on_diagonal(count), jnp.broadcast_to(column, (count, count)), 0.0), axis=0, keepdims=True)


def reduce_kernel(
    devices,
    groups,
    dense_ref,
    cross_ref,
    field_ref,
    weight_ref,
    bias_ref,
    total_ref,
    mean_ref,
    paired,
    summed,
    landed,
    own_sums,
    other_sums,
    own_mean,
    other_mean,
    pair_send,
    pair_recv,
    share_send,
    share_recv,
    sum_send,
    sum_recv,
    mean_send,
    mean_recv,
):
    me = lax.axis_index("pb")
    group = lax.axis_index("walk")
    walkers = weight_ref.shape[1]

    def pb_peer(step):
        return {"pb": lax.rem(me + step, devices)}

    def walk_peer(step):
        return {"walk": lax.rem(group + step, groups)}

    barrier = pltpu.get_barrier_semaphore()
    for step in range(1, devices):
        pl.semaphore_signal(barrier, inc=1, device_id=pb_peer(step), device_id_type=pl.DeviceIdType.MESH)
    for step in range(1, groups):
        pl.semaphore_signal(barrier, inc=1, device_id=walk_peer(step), device_id_type=pl.DeviceIdType.MESH)
    pl.semaphore_wait(barrier, devices + groups - 2)

    def send_all(source_of, target, send_sems, recv_sems, peer, count):
        copies = []
        for step in range(1, count):
            copy = pltpu.make_async_remote_copy(
                src_ref=source_of(step),
                dst_ref=target.at[step - 1],
                send_sem=send_sems.at[step - 1],
                recv_sem=recv_sems.at[step - 1],
                device_id=peer(step),
                device_id_type=pl.DeviceIdType.MESH,
            )
            copy.start()
            copies.append(copy)
        return copies

    parity, line = lax.rem(me, 2), me // 2
    lines = devices // 2
    order = [lines // 2] + [step for step in range(1, lines) if step != lines // 2] + [0]
    pairs = {}
    for step in order:
        target = lax.rem(line + step, lines)
        pairs[step] = pltpu.make_async_remote_copy(
            src_ref=dense_ref.at[2 * target + 1 - parity],
            dst_ref=paired.at[step],
            send_sem=pair_send.at[step],
            recv_sem=pair_recv.at[step],
            device_id={"pb": 2 * line + 1 - parity},
            device_id_type=pl.DeviceIdType.MESH,
        )
        pairs[step].start()
    shares = {}
    for step in order[:-1]:
        owner = 2 * lax.rem(line + step, lines) + parity
        pairs[step].wait_recv()
        summed[step - 1] = dense_ref[owner] + paired[step]
        shares[step] = pltpu.make_async_remote_copy(
            src_ref=summed.at[step - 1],
            dst_ref=landed.at[step - 1],
            send_sem=share_send.at[step - 1],
            recv_sem=share_recv.at[step - 1],
            device_id={"pb": owner},
            device_id_type=pl.DeviceIdType.MESH,
        )
        shares[step].start()
    weight = column_of(weight_ref[...])
    pairs[0].wait_recv()
    real = dense_ref[me, 0] + paired[0, 0]
    imag = dense_ref[me, 1] + paired[0, 1]
    for step in range(1, lines):
        shares[step].wait_recv()
        real = real + landed[step - 1, 0]
        imag = imag + landed[step - 1, 1]
    bias_ref[0] = real
    bias_ref[1] = imag
    shift_real = SQRT_STEP * real
    shift_imag = SQRT_STEP * imag
    field = field_ref[...]
    coulomb = 0.5 * jnp.sum(real * real - imag * imag, axis=1, keepdims=True)
    real_arg = jnp.sum(
        field * shift_real - 0.5 * (shift_real * shift_real - shift_imag * shift_imag), axis=1, keepdims=True
    )
    imag_arg = jnp.sum(field * shift_imag - shift_real * shift_imag, axis=1, keepdims=True)
    lane = lax.broadcasted_iota(jnp.int32, own_sums.shape, 1)
    energy_part = coulomb - 0.5 * cross_ref[...]
    packed = jnp.where(lane == 0, energy_part, jnp.where(lane == 1, real_arg, jnp.where(lane == 2, imag_arg, 0.0)))
    own_sums[...] = packed
    sums = send_all(lambda step: own_sums, other_sums, sum_send, sum_recv, pb_peer, devices)
    for step in range(1, devices):
        sums[step - 1].wait_recv()
    total = jnp.zeros_like(packed)
    for index in range(devices):
        step = lax.rem(me + devices - index, devices)
        arrived = other_sums[jnp.maximum(step - 1, 0)]
        total = total + jnp.where(step == 0, packed, arrived)
    total_ref[...] = total
    energy = jnp.sum(jnp.where(lane == 0, total, 0.0), axis=1, keepdims=True)
    weighted = jnp.sum(weight * energy, axis=0, keepdims=True)
    weights = jnp.sum(weight, axis=0, keepdims=True)
    lane = lax.broadcasted_iota(jnp.int32, own_mean.shape, 1)
    mean = jnp.where(lane == 0, weighted, jnp.where(lane == 1, weights, 0.0))
    own_mean[...] = mean
    means = send_all(lambda step: own_mean, other_mean, mean_send, mean_recv, walk_peer, groups)
    for step in range(1, groups):
        means[step - 1].wait_recv()
    total = jnp.zeros_like(mean)
    for index in range(groups):
        step = lax.rem(group + groups - index, groups)
        arrived = other_mean[jnp.maximum(step - 1, 0)]
        total = total + jnp.where(step == 0, mean, arrived)
    mean_ref[...] = total
    for copy in list(pairs.values()) + list(shares.values()) + sums + means:
        copy.wait_send()


def finish_kernel(sums_ref, total_ref, mean_ref, weight_ref, bias_ref, energy_ref, new_ref, mixed_ref):
    bias_ref[:, 0, :] = sums_ref[0]
    bias_ref[:, 1, :] = sums_ref[1]
    total = total_ref[...]
    weight = column_of(weight_ref[...])
    lane = lax.broadcasted_iota(jnp.int32, total.shape, 1)
    energy = jnp.sum(jnp.where(lane == 0, total, 0.0), axis=1, keepdims=True)
    real = jnp.sum(jnp.where(lane == 1, total, 0.0), axis=1, keepdims=True)
    imag = jnp.sum(jnp.where(lane == 2, total, 0.0), axis=1, keepdims=True)
    energy_ref[...] = row_from(energy)
    new_ref[...] = row_from(weight * jnp.exp(real) * jnp.maximum(jnp.cos(imag), 0.0))
    mean = mean_ref[:1, :]
    mixed_ref[...] = mean[:, 0:1] / mean[:, 1:2]


def local(greens, cholesky, slot_source, block_transfer_index, slot_multiplicity, fields, weight):
    devices = lax.axis_size("pb")
    groups = lax.axis_size("walk")
    me = lax.axis_index("pb")
    walkers, kpoints, flat = greens.shape
    slots, vectors, _ = cholesky.shape
    width = TRANSFER_COUNT * vectors // devices
    vmem = pl.BlockSpec(memory_space=pltpu.VMEM)
    smem = pl.BlockSpec(memory_space=pltpu.SMEM)

    outgoing = pl.pallas_call(
        functools.partial(select_kernel, devices),
        out_shape=(jax.ShapeDtypeStruct((walkers, flat), greens.dtype),) * slots,
        in_specs=[smem, vmem],
        out_specs=(vmem,) * slots,
        scratch_shapes=[pltpu.VMEM((walkers, kpoints, flat), F32), pltpu.VMEM((slots, walkers, flat), F32)],
        compiler_params=pltpu.CompilerParams(vmem_limit_bytes=VMEM_LIMIT),
        name="select",
    )(slot_source, greens)

    arrived = [outgoing[0]]
    for slot in range(1, slots):
        by = devices - offsets_of(devices)[slot]
        arrived.append(lax.ppermute(outgoing[slot], "pb", [(i, (i + by) % devices) for i in range(devices)]))

    rows = 2 * OCCUPIED_COUNT * walkers
    dense, cross = pl.pallas_call(
        compute_kernel,
        grid=(slots,),
        out_shape=(
            jax.ShapeDtypeStruct((devices, 2, walkers, width), F32),
            jax.ShapeDtypeStruct((walkers, 1), F32),
        ),
        in_specs=[
            smem,
            smem,
            pl.BlockSpec((1, vectors, flat), lambda s: (s, 0, 0)),
            pl.BlockSpec((2, WINDOW, 4 * WINDOW), lambda s: (0, 0, 0)),
        ]
        + [pl.BlockSpec((walkers, flat), lambda s: (0, 0))] * slots,
        out_specs=(
            pl.BlockSpec((devices, 2, walkers, width), lambda s: (0, 0, 0, 0)),
            pl.BlockSpec((walkers, 1), lambda s: (0, 0)),
        ),
        scratch_shapes=[
            pltpu.VMEM((2, rows, WINDOW), greens.dtype),
            pltpu.VMEM((OCCUPIED_COUNT, rows, vectors // WINDOW * WINDOW + LANES), F32),
            pltpu.VMEM((slots, 2, walkers, vectors), F32),
            pltpu.VMEM((walkers, vectors), F32),
            pltpu.VMEM((walkers, flat), greens.dtype),
            pltpu.VMEM((2, LANES * OCCUPIED_COUNT // 2, WINDOW), greens.dtype),
        ],
        compiler_params=pltpu.CompilerParams(
            dimension_semantics=("arbitrary",), vmem_limit_bytes=VMEM_LIMIT
        ),
        name="terms",
    )(block_transfer_index, slot_multiplicity, cholesky, jnp.asarray(arrangement(), greens.dtype), *arrived)

    if width % vectors == 0:
        each = width // vectors
        field_share = lax.dynamic_slice_in_dim(fields, me * each, each, 1).reshape(walkers, width)
    else:
        flat_fields = fields.reshape(walkers, TRANSFER_COUNT * vectors)
        field_share = lax.dynamic_slice_in_dim(flat_fields, me * width, width, 1)

    sums, total, mean = pl.pallas_call(
        functools.partial(reduce_kernel, devices, groups),
        out_shape=(
            jax.ShapeDtypeStruct((2, walkers, width), F32),
            jax.ShapeDtypeStruct((walkers, 128), F32),
            jax.ShapeDtypeStruct((8, 128), F32),
        ),
        in_specs=[vmem] * 4,
        out_specs=(vmem,) * 3,
        scratch_shapes=[
            pltpu.VMEM((devices // 2, 2, walkers, width), F32),
            pltpu.VMEM((devices // 2 - 1, 2, walkers, width), F32),
            pltpu.VMEM((devices // 2 - 1, 2, walkers, width), F32),
            pltpu.VMEM((walkers, 128), F32),
            pltpu.VMEM((devices - 1, walkers, 128), F32),
            pltpu.VMEM((8, 128), F32),
            pltpu.VMEM((groups - 1, 8, 128), F32),
            pltpu.SemaphoreType.DMA((devices // 2,)),
            pltpu.SemaphoreType.DMA((devices // 2,)),
            pltpu.SemaphoreType.DMA((devices // 2 - 1,)),
            pltpu.SemaphoreType.DMA((devices // 2 - 1,)),
            pltpu.SemaphoreType.DMA((devices - 1,)),
            pltpu.SemaphoreType.DMA((devices - 1,)),
            pltpu.SemaphoreType.DMA((groups - 1,)),
            pltpu.SemaphoreType.DMA((groups - 1,)),
        ],
        compiler_params=pltpu.CompilerParams(collective_id=1, has_side_effects=True, vmem_limit_bytes=VMEM_LIMIT),
        name="reduce",
    )(dense, cross, field_share, weight.reshape(1, walkers))

    bias, energy, new_weight, mixed = pl.pallas_call(
        finish_kernel,
        out_shape=(
            jax.ShapeDtypeStruct((walkers, 2, width), F32),
            jax.ShapeDtypeStruct((1, walkers), F32),
            jax.ShapeDtypeStruct((1, walkers), F32),
            jax.ShapeDtypeStruct((1, 1), F32),
        ),
        in_specs=[vmem] * 4,
        out_specs=(vmem,) * 4,
        name="finish",
    )(sums, total, mean, weight.reshape(1, walkers))
    return (bias, energy.reshape(walkers), new_weight.reshape(walkers), mixed.reshape(()))


def solution(mesh):
    placed = (
        P("walk", "pb", None),
        P("pb", None, None),
        P(),
        P("pb"),
        P("pb"),
        P("walk", None, None),
        P("walk"),
    )
    return jax.shard_map(
        local,
        mesh=mesh,
        in_specs=placed,
        out_specs=(P("walk", None, "pb"), P("walk"), P("walk"), P()),
        check_vma=False,
    )
```

profile of v0, /device:TPU:0, one launch (start us, length us, event | category | flops | bytes accessed | tf_op | source)
XLA Modules:
  0.0 56.6 jit_solution(9582072653688411471)
XLA Ops:
  0.6 0.0 copy-start
  0.6 2.2 %select.1 = (bf16[16,3072]{1,0:T(8,128)(2,1)}, bf16[16,3072]{1,0:T(8,128)(2,1)}, bf16[16,3072]{1,0:T(8,128)(2,1)}, bf16[16,3072]{1,0:T(8,128)(2,1)}) custom-call(s32[32]{0:T(128)} %source_ref.1, bf16[16,8,3072]{2,1,0:T(8,128)(2,1)} %greens_ref.1), custom_call_target="tpu_custom_call" | custom-call | tf_op jit(solution)/shard_map/select/pallas_call | solution.py:342
  2.9 3.0 %collective-permute-start = (bf16[16,3072]{1,0:T(8,128)(2,1)}, bf16[16,3072]{1,0:T(8,128)(2,1)S(1)}, u32[]{:S(2)}, u32[]{:S(2)}) collective-permute-start(bf16[16,3072]{1,0:T(8,128)(2,1)} %get-tuple-element.18), channel_id=1, source_target_pairs={{0,1},{1,2},{2,3},{3,4},{4,5},{5,6},{6,7},{7,0},{8,9},{9,10},{10,1... | collective-permute-start | bytes 294920 | tf_op jit(solution)/shard_map/ppermute | solution.py:355
  5.9 3.0 %collective-permute-start.1 = (bf16[16,3072]{1,0:T(8,128)(2,1)}, bf16[16,3072]{1,0:T(8,128)(2,1)S(1)}, u32[]{:S(2)}, u32[]{:S(2)}) collective-permute-start(bf16[16,3072]{1,0:T(8,128)(2,1)} %get-tuple-element.19), channel_id=1, source_target_pairs={{0,7},{1,0},{2,1},{3,2},{4,3},{5,4},{6,5},{7,6},{8,15},{9,8},{10,9... | collective-permute-start | bytes 294920 | tf_op jit(solution)/shard_map/ppermute | solution.py:355
  8.9 1.0 %collective-permute-start.2 = (bf16[16,3072]{1,0:T(8,128)(2,1)}, bf16[16,3072]{1,0:T(8,128)(2,1)S(1)}, u32[]{:S(2)}, u32[]{:S(2)}) collective-permute-start(bf16[16,3072]{1,0:T(8,128)(2,1)} %get-tuple-element.20), channel_id=1, source_target_pairs={{0,4},{1,5},{2,6},{3,7},{4,0},{5,1},{6,2},{7,3},{8,12},{9,13},{10,... | collective-permute-start | bytes 294920 | tf_op jit(solution)/shard_map/ppermute | solution.py:355
  9.8 8.3 %copy.13.chol_ref = bf16[4,300,3072]{2,1,0:T(8,128)(2,1)} copy(bf16[4,300,3072]{2,0,1:T(4,128)(2,1)} %param.9) | data formatting | bytes 14745600 | tf_op args[1]
  18.2 0.0 copy-done
  18.2 0.7 %reshape.24.field_ref = f32[16,600]{1,0:T(8,128)} reshape(f32[16,2,300]{2,1,0:T(2,128)S(1)} %constant_dynamic-slice_fusion) | data formatting | bytes 76800 | tf_op jit(solution)/shard_map/reshape | solution.py:392
  18.9 0.0 collective-permute-done.rest_1_
  18.9 0.0 copy-start.1
  18.9 0.0 collective-permute-done.1.rest_2_
  18.9 0.0 copy-start.2
  18.9 0.0 collective-permute-done.2.rest_3_
  19.0 0.0 copy-start.3
  19.0 0.6 %copy-done.1 = bf16[16,3072]{1,0:T(8,128)(2,1)} copy-done((bf16[16,3072]{1,0:T(8,128)(2,1)}, bf16[16,3072]{1,0:T(8,128)(2,1)S(1)}, u32[]{:S(2)}) %copy-start.1) | copy-done | bytes 98328
  19.6 0.0 copy-done.2
  19.6 0.1 copy-done.3
  19.7 11.9 %terms.1 = (f32[8,2,16,600]{3,2,1,0:T(8,128)}, f32[16,1]{1,0:T(8,128)}) custom-call(s32[4]{0:T(128)} %transfer_ref.1, s32[4]{0:T(128)} %multiple_ref.1, bf16[4,300,3072]{2,1,0:T(8,128)(2,1)} %copy.13.chol_ref, bf16[2,256,1024]{2,1,0:T(8,128)(2,1)} %constant.12.clone.table_ref, bf16[16,3072]{1,0:T(8,128)(2,1)} %get-tuple-element.17.rest_0_, ...), custom_call_target="tpu_custom_call" | custom-call | tf_op jit(solution)/shard_map/terms/pallas_call | solution.py:358
  31.6 23.4 %reduce.1 = (f32[2,16,600]{2,1,0:T(8,128)}, f32[16,128]{1,0:T(8,128)}, f32[8,128]{1,0:T(8,128)}) custom-call(f32[8,2,16,600]{3,2,1,0:T(8,128)} %get-tuple-element.21.dense_ref, f32[16,1]{1,0:T(8,128)} %get-tuple-element.22.cross_ref, f32[16,600]{1,0:T(8,128)} %reshape.24.field_ref, f32[1,16]{1,0:T(1,128)} %bitcast.4), custom_call_target="tpu_custom_call" | custom-call | tf_op jit(solution)/shard_map/reduce/pallas_call | solution.py:397
  55.0 1.7 %finish.1 = (f32[16,2,600]{2,1,0:T(2,128)}, f32[1,16]{1,0:T(1,128)}, f32[1,16]{1,0:T(1,128)}, f32[1,1]{1,0:T(1,128)}) custom-call(f32[2,16,600]{2,1,0:T(8,128)} %get-tuple-element.23.sums_ref, f32[16,128]{1,0:T(8,128)} %get-tuple-element.24.total_ref, f32[8,128]{1,0:T(8,128)} %get-tuple-element.25.mean_ref, f32[1,16]{1,0:T(1,128)} %bitcast.5), custom_call_target="tpu_custom_call" | custom-call | tf_op jit(solution)/shard_map/finish/pallas_call | solution.py:427
  (1 shorter events, 0.0 us)
Async XLA Ops:
  0.6 17.6 %copy-start = (f32[16,16,300]{2,1,0:T(8,128)S(1)}, f32[16,16,300]{2,1,0:T(8,128)}, u32[]{:S(2)}) copy-start(f32[16,16,300]{2,1,0:T(8,128)} %param.13) | copy-start | bytes 921604
  2.9 16.1 %collective-permute-start = (bf16[16,3072]{1,0:T(8,128)(2,1)}, bf16[16,3072]{1,0:T(8,128)(2,1)S(1)}, u32[]{:S(2)}, u32[]{:S(2)}) collective-permute-start(bf16[16,3072]{1,0:T(8,128)(2,1)} %get-tuple-element.18), channel_id=1, source_target_pairs={{0,1},{1,2},{2,3},{3,4},{4,5},{5,6},{6,7},{7,0},{8,9},{9,10},{10,1... | collective-permute-start | bytes 294920 | tf_op jit(solution)/shard_map/ppermute | solution.py:355
  5.9 13.1 %collective-permute-start.1 = (bf16[16,3072]{1,0:T(8,128)(2,1)}, bf16[16,3072]{1,0:T(8,128)(2,1)S(1)}, u32[]{:S(2)}, u32[]{:S(2)}) collective-permute-start(bf16[16,3072]{1,0:T(8,128)(2,1)} %get-tuple-element.19), channel_id=1, source_target_pairs={{0,7},{1,0},{2,1},{3,2},{4,3},{5,4},{6,5},{7,6},{8,15},{9,8},{10,9... | collective-permute-start | bytes 294920 | tf_op jit(solution)/shard_map/ppermute | solution.py:355
  8.9 10.1 %collective-permute-start.2 = (bf16[16,3072]{1,0:T(8,128)(2,1)}, bf16[16,3072]{1,0:T(8,128)(2,1)S(1)}, u32[]{:S(2)}, u32[]{:S(2)}) collective-permute-start(bf16[16,3072]{1,0:T(8,128)(2,1)} %get-tuple-element.20), channel_id=1, source_target_pairs={{0,4},{1,5},{2,6},{3,7},{4,0},{5,1},{6,2},{7,3},{8,12},{9,13},{10,... | collective-permute-start | bytes 294920 | tf_op jit(solution)/shard_map/ppermute | solution.py:355
  18.9 0.7 %copy-start.1 = (bf16[16,3072]{1,0:T(8,128)(2,1)}, bf16[16,3072]{1,0:T(8,128)(2,1)S(1)}, u32[]{:S(2)}) copy-start(bf16[16,3072]{1,0:T(8,128)(2,1)S(1)} %collective-permute-done.rest_1_) | copy-start | bytes 294916
  18.9 0.7 %copy-start.2 = (bf16[16,3072]{1,0:T(8,128)(2,1)}, bf16[16,3072]{1,0:T(8,128)(2,1)S(1)}, u32[]{:S(2)}) copy-start(bf16[16,3072]{1,0:T(8,128)(2,1)S(1)} %collective-permute-done.1.rest_2_) | copy-start | bytes 294916
  19.0 0.7 %copy-start.3 = (bf16[16,3072]{1,0:T(8,128)(2,1)}, bf16[16,3072]{1,0:T(8,128)(2,1)S(1)}, u32[]{:S(2)}) copy-start(bf16[16,3072]{1,0:T(8,128)(2,1)S(1)} %collective-permute-done.2.rest_3_) | copy-start | bytes 294916
where the time goes:
time: 56.9 us; the launch traced here: 56.6 us
  Pallas kernels  39.2 us (69%)
  local copies, waits for them, and re-layouts  9.78 us (17%)
  starting transfers between devices  6.99 us (12%)
  between operations  0.68 us (1%)
    pallas_call x1, Pallas kernels, local(): pl.pallas_call(functools.partial(reduce_kernel, devices, groups), out_sha...  23.4 us
    pallas_call x1, Pallas kernels, local(): pl.pallas_call(compute_kernel, grid=(slots,), out_shape=(jax.ShapeDtypeSt...  11.9 us
    unnamed x9, local copies, waits for them, and re-layouts  9.05 us
    ppermute x3, starting transfers between devices, local(): lax.ppermute(outgoing[slot], 'pb', [(i, (i + by) % devices) for i in rang...  6.99 us
    pallas_call x1, Pallas kernels, local(): pl.pallas_call(functools.partial(select_kernel, devices), out_shape=(jax....  2.21 us
    pallas_call x1, Pallas kernels, local(): pl.pallas_call(finish_kernel, out_shape=(jax.ShapeDtypeStruct((walkers, 2...  1.65 us
  transfers between devices with their start and end apart: 3, of which 0 were waited for; matrix products, arithmetic and copies ran while one was open for 16% of the time, Pallas kernels for 0%

commit v1 on v0

v1 whole, which is shorter than its diff:
```python
import functools

import jax
import jax.numpy as jnp
from jax import lax
from jax.experimental import pallas as pl
from jax.experimental.pallas import tpu as pltpu
from jax.sharding import PartitionSpec as P

ORBITAL_COUNT = 96
OCCUPIED_COUNT = 16
TRANSFER_COUNT = 16
SQRT_STEP = 0.05

DOUBLED = 2 * ORBITAL_COUNT
PAIR = 2 * DOUBLED
WINDOW = 256
SHIFT = PAIR - WINDOW
LANES = 128
BLOCK = 16
VMEM_LIMIT = 60 * 1024 * 1024
F32 = jnp.float32
MESH = pl.DeviceIdType.MESH


def offsets_of(devices):
    return [0, devices - 1, 1, devices // 2]


def row_of(part, occupied, walkers):
    half = (OCCUPIED_COUNT // 2) * walkers
    return part * 2 * half + (occupied % 2) * half + (occupied // 2) * walkers


def on_diagonal(count):
    return lax.broadcasted_iota(jnp.int32, (count, count), 0) == lax.broadcasted_iota(jnp.int32, (count, count), 1)


def column_of(row):
    count = row.shape[1]
    return jnp.sum(jnp.where(on_diagonal(count), jnp.broadcast_to(row, (count, count)), 0.0), axis=1, keepdims=True)


def row_from(column):
    count = column.shape[0]
    return jnp.sum(jnp.where(on_diagonal(count), jnp.broadcast_to(column, (count, count)), 0.0), axis=0, keepdims=True)


def step_kernel(
    devices,
    groups,
    source_ref,
    transfer_ref,
    multiple_ref,
    greens_hbm,
    chol_hbm,
    fields_hbm,
    weight_ref,
    bias_ref,
    energy_ref,
    new_ref,
    mixed_ref,
    greens,
    fields,
    raw,
    wide,
    chol,
    picked,
    arrived,
    dense_left,
    operand,
    product,
    tails,
    crossed,
    mine,
    theirs,
    rows_of_field,
    linear,
    summed,
    landed,
    own_sums,
    other_sums,
    own_mean,
    other_mean,
    local_sem,
    green_send,
    green_recv,
    pair_send,
    pair_recv,
    share_send,
    share_recv,
    sum_send,
    sum_recv,
    mean_send,
    mean_recv,
):
    me = lax.axis_index("pb")
    group = lax.axis_index("walk")
    slots, _, walkers, _ = mine.shape
    vectors = chol_hbm.shape[0]
    per_vector = chol_hbm.shape[1]
    kpoints = greens.shape[0] // walkers
    tiles = per_vector // slots
    pairs = OCCUPIED_COUNT // 2
    lines = devices // 2
    parity, line = lax.rem(me, 2), me // 2
    width = bias_ref.shape[2]
    offsets = offsets_of(devices)

    def pb_peer(step):
        return {"pb": lax.rem(me + step, devices)}

    def walk_peer(step):
        return {"walk": lax.rem(group + step, groups)}

    barrier = pltpu.get_barrier_semaphore()
    for step in range(1, devices):
        pl.semaphore_signal(barrier, inc=1, device_id=pb_peer(step), device_id_type=MESH)
    for step in range(1, groups):
        pl.semaphore_signal(barrier, inc=1, device_id=walk_peer(step), device_id_type=MESH)

    green_in = pltpu.make_async_copy(greens_hbm, greens, local_sem.at[0])
    green_in.start()
    chunk = -(-vectors // (4 * BLOCK)) * BLOCK
    pieces = []
    for number, first in enumerate(range(0, vectors, chunk)):
        count = min(chunk, vectors - first)
        piece = pltpu.make_async_copy(
            chol_hbm.at[pl.ds(first, count)], raw.at[pl.ds(first, count)], local_sem.at[2 + number]
        )
        piece.start()
        pieces.append((first, count, piece))
    field_in = pltpu.make_async_copy(fields_hbm, fields, local_sem.at[1])
    field_in.start()

    green_in.wait()
    lane = lax.broadcasted_iota(jnp.int32, (walkers, walkers * kpoints), 1)
    row = lax.broadcasted_iota(jnp.int32, (walkers, walkers * kpoints), 0)
    chosen = []
    for slot in range(slots):
        requester = lax.rem(me + devices - offsets[slot], devices)
        index = lax.rem(source_ref[requester * slots + slot], kpoints)
        chosen.append(jnp.where(lane == row * kpoints + index, 1.0, 0.0))
    chosen = jnp.concatenate(chosen, 0).astype(greens.dtype)
    flat = greens.shape[1]
    span = PAIR * 2
    for first in range(0, flat, span):
        rows = jnp.dot(chosen, greens[:, first : first + span], preferred_element_type=F32).astype(greens.dtype)
        arrived[0, :, first : first + span] = rows[:walkers]
        for slot in range(1, slots):
            picked[slot - 1, :, first : first + span] = rows[slot * walkers : (slot + 1) * walkers]

    pl.semaphore_wait(barrier, devices + groups - 2)

    def green_copy(slot):
        return pltpu.make_async_remote_copy(
            src_ref=picked.at[slot - 1],
            dst_ref=arrived.at[slot],
            send_sem=green_send.at[slot - 1],
            recv_sem=green_recv.at[slot - 1],
            device_id=pb_peer(devices - offsets[slot] if slot else 0),
            device_id_type=MESH,
        )

    for slot in range(1, slots):
        green_copy(slot).start()

    def split(block, carry):
        first = pl.multiple_of(block * BLOCK, BLOCK)
        for n in range(BLOCK):
            wide[n * per_vector : (n + 1) * per_vector, :] = raw[first + n].astype(F32)
        for slot in range(slots):
            for tile in range(tiles):
                part = wide[pl.ds(tile * slots + slot, BLOCK, stride=per_vector), :]
                chol[slot, pl.ds(first, BLOCK), tile * LANES : (tile + 1) * LANES] = part.astype(chol.dtype)
        return carry

    for first, count, piece in pieces:
        piece.wait()
        lax.fori_loop(first // BLOCK, -(-(first + count) // BLOCK), split, 0)
    field_in.wait()
    tails[...] = jnp.zeros_like(tails)
    linear[...] = jnp.zeros_like(linear)
    crossed[...] = jnp.zeros_like(crossed)

    pair_lane = lax.broadcasted_iota(jnp.int32, (walkers, PAIR), 1)
    is_real = lax.rem(pair_lane, DOUBLED) < ORBITAL_COUNT
    window_lane = lax.broadcasted_iota(jnp.int32, (walkers, WINDOW), 1)

    def arranged(slot, p):
        both = arrived[slot, :, PAIR * p : PAIR * (p + 1)].astype(F32)
        real = jnp.where(is_real, both, -both)
        imag = jnp.where(is_real, pltpu.roll(both, PAIR - ORBITAL_COUNT, 1), pltpu.roll(both, ORBITAL_COUNT, 1))
        return real, imag

    def pair_copy(slot):
        return pltpu.make_async_remote_copy(
            src_ref=mine.at[slot],
            dst_ref=theirs.at[slot],
            send_sem=pair_send.at[slot],
            recv_sem=pair_recv.at[slot],
            device_id={"pb": 2 * line + 1 - parity},
            device_id_type=MESH,
        )

    def traces(slot):
        for p in range(pairs):
            for part, value in enumerate(arranged(slot, p)):
                dense_left[part * walkers : (part + 1) * walkers, PAIR * p : PAIR * (p + 1)] = value.astype(
                    dense_left.dtype
                )
        trace = lax.dot_general(
            dense_left[...], chol[slot, :vectors, :], (((1,), (1,)), ((), ())), preferred_element_type=F32
        )
        trace = trace * multiple_ref[slot].astype(F32)
        transfer = transfer_ref[slot]
        for w in range(walkers):
            rows_of_field[w : w + 1, :] = fields[w, pl.ds(transfer, 1), :]
        mark = jnp.full((walkers, mine.shape[3]), transfer.astype(F32))
        for part in range(2):
            value = trace[part * walkers : (part + 1) * walkers]
            mine[slot, part] = mark
            mine[slot, part, :, :vectors] = value
            linear[part] += rows_of_field[...] * value
        pair_copy(slot).start()

    main = vectors // WINDOW * WINDOW
    rest_count = vectors - main

    def window_of(i):
        start = PAIR * (i // 2) + SHIFT * (i % 2)
        return slice(start, start + WINDOW)

    def exchange(slot):
        for p in range(pairs):
            for part, value in enumerate(arranged(slot, p)):
                low, high = value[:, :WINDOW], value[:, SHIFT:]
                even, odd = row_of(part, 2 * p, walkers), row_of(part, 2 * p + 1, walkers)
                last = WINDOW - DOUBLED
                operand[0, even : even + walkers, :] = jnp.where(window_lane < DOUBLED, low, 0.0).astype(operand.dtype)
                operand[1, even : even + walkers, :] = jnp.where(
                    window_lane >= last, pltpu.roll(low, last, 1), 0.0
                ).astype(operand.dtype)
                operand[0, odd : odd + walkers, :] = jnp.where(
                    window_lane < DOUBLED, pltpu.roll(high, DOUBLED, 1), 0.0
                ).astype(operand.dtype)
                operand[1, odd : odd + walkers, :] = jnp.where(window_lane >= last, high, 0.0).astype(operand.dtype)

        def times(which, right):
            return lax.dot_general(operand[which], right, (((1,), (1,)), ((), ())), preferred_element_type=F32)

        for i in range(OCCUPIED_COUNT):
            tails[i % 2, pl.ds(LANES * (i // 2), rest_count), :] = chol[slot, main:vectors, window_of(i)]
        for which in range(2):
            ends = times(which, tails[which])
            for p in range(pairs):
                product[2 * p + which, :, main : main + LANES] = ends[:, LANES * p : LANES * (p + 1)]

        def multiply(i):
            product[i, :, :main] = times(i % 2, chol[slot, :main, window_of(i)])

        def block(i, j, part):
            return product[i, pl.ds(row_of(part, j, walkers), walkers), :]

        zero = jnp.zeros((walkers, main + LANES), F32)
        off = [zero, zero]
        own = [zero, zero]
        multiply(0)
        for i in range(OCCUPIED_COUNT):
            if i + 1 < OCCUPIED_COUNT:
                multiply(i + 1)
            for part in range(2):
                here = block(i, i, part)
                own[part] = own[part] + here * here
                for j in range(i):
                    off[part] = off[part] + block(i, j, part) * block(j, i, part)
        crossed[...] += multiple_ref[slot].astype(F32) * ((own[0] - own[1]) + 2.0 * (off[0] - off[1]))[:, :vectors]

    def share_copy(step):
        owner = 2 * lax.rem(line + step, lines) + parity
        return pltpu.make_async_remote_copy(
            src_ref=summed.at[step],
            dst_ref=landed.at[step - 1],
            send_sem=share_send.at[step - 1],
            recv_sem=share_recv.at[step - 1],
            device_id={"pb": owner},
            device_id_type=MESH,
        )

    def terms_of(transfer, part):
        value = jnp.zeros((walkers, vectors), F32)
        for held in (mine, theirs):
            for slot in range(slots):
                here = held[slot, part]
                value = value + jnp.where(here[:, vectors : vectors + 1] == transfer, here[:, :vectors], 0.0)
        return value

    def share_of(step):
        owner = 2 * lax.rem(line + step, lines) + parity
        for part in range(2):
            if width % vectors == 0:
                each = width // vectors
                for index in range(each):
                    value = terms_of((owner * each + index).astype(F32), part)
                    summed[step, part, :, index * vectors : (index + 1) * vectors] = value
            else:
                per = vectors // width
                value = terms_of((owner // per).astype(F32), part)
                piece = lax.rem(owner, per)
                taken = value[:, :width]
                for index in range(1, per):
                    taken = jnp.where(piece == index, value[:, index * width : (index + 1) * width], taken)
                summed[step, part] = taken

    order = [lines // 2] + [step for step in range(1, lines) if step != lines // 2]

    def round_of(slot, carry):
        @pl.when(slot == 0)
        def _():
            traces(0)

        @pl.when(slot == 1)
        def _():
            for other in range(1, slots):
                green_copy(other).wait_recv()

            def one(other, inner):
                traces(other)
                return inner

            lax.fori_loop(1, slots, one, 0)

        exchange(slot)

        @pl.when(slot == 1)
        def _():
            for held in range(slots):
                pair_copy(held).wait_recv()
            for step in order:
                share_of(step)
                share_copy(step).start()
            share_of(0)

        return carry

    lax.fori_loop(0, slots, round_of, 0)

    weight = column_of(weight_ref[...])
    real = summed[0, 0]
    imag = summed[0, 1]
    for step in range(1, lines):
        share_copy(step).wait_recv()
        real = real + landed[step - 1, 0]
        imag = imag + landed[step - 1, 1]
    bias_ref[:, 0, :] = real
    bias_ref[:, 1, :] = imag
    coulomb = jnp.sum(real * real - imag * imag, axis=1, keepdims=True)
    mixed_part = jnp.sum(real * imag, axis=1, keepdims=True)
    square = SQRT_STEP * SQRT_STEP
    real_arg = SQRT_STEP * jnp.sum(linear[0], axis=1, keepdims=True) - (0.5 * square) * coulomb
    imag_arg = SQRT_STEP * jnp.sum(linear[1], axis=1, keepdims=True) - square * mixed_part
    energy_part = 0.5 * coulomb - 0.5 * jnp.sum(crossed[...], axis=1, keepdims=True)
    lane = lax.broadcasted_iota(jnp.int32, own_sums.shape, 1)
    packed = jnp.where(lane == 0, energy_part, jnp.where(lane == 1, real_arg, jnp.where(lane == 2, imag_arg, 0.0)))
    own_sums[...] = packed

    def send_all(source, target, send_sems, recv_sems, peer, count):
        copies = []
        for step in range(1, count):
            copy = pltpu.make_async_remote_copy(
                src_ref=source,
                dst_ref=target.at[step - 1],
                send_sem=send_sems.at[step - 1],
                recv_sem=recv_sems.at[step - 1],
                device_id=peer(step),
                device_id_type=MESH,
            )
            copy.start()
            copies.append(copy)
        return copies

    sums = send_all(own_sums, other_sums, sum_send, sum_recv, pb_peer, devices)
    for copy in sums:
        copy.wait_recv()
    total = jnp.zeros_like(packed)
    for index in range(devices):
        step = lax.rem(me + devices - index, devices)
        total = total + jnp.where(step == 0, packed, other_sums[jnp.maximum(step - 1, 0)])
    energy = total[:, 0:1]
    weighted = jnp.sum(weight * energy, axis=0, keepdims=True)
    weights = jnp.sum(weight, axis=0, keepdims=True)
    lane = lax.broadcasted_iota(jnp.int32, own_mean.shape, 1)
    mean = jnp.where(lane == 0, weighted, jnp.where(lane == 1, weights, 0.0))
    own_mean[...] = mean
    means = send_all(own_mean, other_mean, mean_send, mean_recv, walk_peer, groups)
    energy_ref[...] = row_from(energy)
    new_ref[...] = row_from(weight * jnp.exp(total[:, 1:2]) * jnp.maximum(jnp.cos(total[:, 2:3]), 0.0))
    for copy in means:
        copy.wait_recv()
    total = jnp.zeros_like(mean)
    for index in range(groups):
        step = lax.rem(group + groups - index, groups)
        total = total + jnp.where(step == 0, mean, other_mean[jnp.maximum(step - 1, 0)])
    mixed_ref[...] = total[0:1, 0:1] / total[0:1, 1:2]
    for slot in range(1, slots):
        green_copy(slot).wait_send()
    for slot in range(slots):
        pair_copy(slot).wait_send()
    for step in range(1, lines):
        share_copy(step).wait_send()
    for copy in sums + means:
        copy.wait_send()


def local(greens, cholesky, slot_source, block_transfer_index, slot_multiplicity, fields, weight):
    devices = lax.axis_size("pb")
    groups = lax.axis_size("walk")
    walkers, kpoints, flat = greens.shape
    slots, vectors, _ = cholesky.shape
    width = TRANSFER_COUNT * vectors // devices
    lines = devices // 2
    tiles = flat // LANES
    padded = -(-vectors // BLOCK) * BLOCK
    lanes = (vectors // LANES + 1) * LANES
    main = vectors // WINDOW * WINDOW
    rows = 2 * OCCUPIED_COUNT * walkers
    half = greens.dtype
    vmem = pl.BlockSpec(memory_space=pltpu.VMEM)
    smem = pl.BlockSpec(memory_space=pltpu.SMEM)
    hbm = pl.BlockSpec(memory_space=pl.ANY)
    dma = pltpu.SemaphoreType.DMA

    by_vector = (
        cholesky.reshape(slots, vectors, tiles, LANES).transpose(1, 2, 0, 3).reshape(vectors, tiles * slots, LANES)
    )
    bias, energy, new_weight, mixed = pl.pallas_call(
        functools.partial(step_kernel, devices, groups),
        out_shape=(
            jax.ShapeDtypeStruct((walkers, 2, width), F32),
            jax.ShapeDtypeStruct((1, walkers), F32),
            jax.ShapeDtypeStruct((1, walkers), F32),
            jax.ShapeDtypeStruct((1, 1), F32),
        ),
        in_specs=[smem, smem, smem, hbm, hbm, hbm, vmem],
        out_specs=(vmem,) * 4,
        scratch_shapes=[
            pltpu.VMEM((walkers * kpoints, flat), half),
            pltpu.VMEM(fields.shape, F32),
            pltpu.VMEM((padded, tiles * slots, LANES), half),
            pltpu.VMEM((BLOCK * tiles * slots, LANES), F32),
            pltpu.VMEM((slots, padded, flat), half),
            pltpu.VMEM((slots - 1, walkers, flat), half),
            pltpu.VMEM((slots, walkers, flat), half),
            pltpu.VMEM((2 * walkers, flat), half),
            pltpu.VMEM((2, rows, WINDOW), half),
            pltpu.VMEM((OCCUPIED_COUNT, rows, main + LANES), F32),
            pltpu.VMEM((2, LANES * OCCUPIED_COUNT // 2, WINDOW), half),
            pltpu.VMEM((walkers, vectors), F32),
            pltpu.VMEM((slots, 2, walkers, lanes), F32),
            pltpu.VMEM((slots, 2, walkers, lanes), F32),
            pltpu.VMEM((walkers, vectors), F32),
            pltpu.VMEM((2, walkers, vectors), F32),
            pltpu.VMEM((lines, 2, walkers, width), F32),
            pltpu.VMEM((lines - 1, 2, walkers, width), F32),
            pltpu.VMEM((walkers, LANES), F32),
            pltpu.VMEM((devices - 1, walkers, LANES), F32),
            pltpu.VMEM((8, LANES), F32),
            pltpu.VMEM((max(groups - 1, 1), 8, LANES), F32),
            dma((8,)),
            dma((slots - 1,)),
            dma((slots - 1,)),
            dma((slots,)),
            dma((slots,)),
            dma((lines - 1,)),
            dma((lines - 1,)),
            dma((devices - 1,)),
            dma((devices - 1,)),
            dma((max(groups - 1, 1),)),
            dma((max(groups - 1, 1),)),
        ],
        compiler_params=pltpu.CompilerParams(collective_id=1, has_side_effects=True, vmem_limit_bytes=VMEM_LIMIT),
        name="step",
    )(
        slot_source,
        block_transfer_index,
        slot_multiplicity,
        greens.reshape(walkers * kpoints, flat),
        by_vector,
        fields,
        weight.reshape(1, walkers),
    )
    return bias, energy.reshape(walkers), new_weight.reshape(walkers), mixed.reshape(())


def solution(mesh):
    placed = (
        P("walk", "pb", None),
        P("pb", None, None),
        P(),
        P("pb"),
        P("pb"),
        P("walk", None, None),
        P("walk"),
    )
    return jax.shard_map(
        local,
        mesh=mesh,
        in_specs=placed,
        out_specs=(P("walk", None, "pb"), P("walk"), P("walk"), P()),
        check_vma=False,
    )
```

time: 56.9 us -> 47.3 us (0.83)
  starting transfers between devices: 6.99 us -> 0 us
  local copies, waits for them, and re-layouts: 9.78 us -> 3.83 us
  Pallas kernels: 39.2 us -> 40.9 us
  between operations: 0.68 us -> 2.33 us
    ppermute x3 -> x0, starting transfers between devices: 6.99 us -> none  [local(): lax.ppermute(outgoing[slot], 'pb', [(i, (i + by) % devices) for i in rang...]
    unnamed x9 -> x3, local copies, waits for them, and re-layouts: 9.05 us -> 3.83 us
    pallas_call x4 -> x1, Pallas kernels: 39.2 us -> 40.9 us  [local(): pl.pallas_call(functools.partial(step_kernel, devices, groups), out_shape...]
    reshape x1 -> x0, local copies, waits for them, and re-layouts: 0.71 us -> none  [local(): lax.dynamic_slice_in_dim(fields, me * each, each, 1).reshape(walkers, width)]
  transfers between devices with their start and end apart: 3 -> 0, of which waited for: 0 -> 0; matrix products, arithmetic and copies ran while one was open for 16% -> 0% of each run, Pallas kernels for 0% -> 0%
where the time goes in v1:
time: 47.3 us; the launch traced here: 47.1 us
  Pallas kernels  40.9 us (86%)
  local copies, waits for them, and re-layouts  3.83 us (8%)
  between operations  2.33 us (5%)
    pallas_call x1, Pallas kernels, local(): pl.pallas_call(functools.partial(step_kernel, devices, groups), out_shape...  40.9 us
    unnamed x3, local copies, waits for them, and re-layouts  3.83 us

profile of v1, /device:TPU:0, one launch (start us, length us, event | category | flops | bytes accessed | tf_op | source)
XLA Modules:
  0.0 47.1 jit_solution(10883322914747915181)
XLA Ops:
  0.6 40.9 %step.1 = (f32[16,2,600]{2,1,0:T(2,128)}, f32[1,16]{1,0:T(1,128)}, f32[1,16]{1,0:T(1,128)}, f32[1,1]{1,0:T(1,128)}) custom-call(s32[32]{0:T(128)} %source_ref.1, s32[4]{0:T(128)} %transfer_ref.1, s32[4]{0:T(128)} %multiple_ref.1, bf16[128,3072]{1,0:T(8,128)(2,1)} %bitcast.11, bf16[300,96,128]{2,1,0:T(8,128)(2,1)} %bitcast.10, f32[16,16,300]{2,1,0:T(8,128)} %fields_hbm.1, ...), custom_call_target="tpu_custom_call" | custom-call | tf_op jit(solution)/shard_map/step/pallas_call | solution.py:436
  41.5 1.5 %copy.16 = f32[16,2,600]{2,1,0:T(2,128)} copy(f32[16,2,600]{2,1,0:T(2,128)} %get-tuple-element.16) | data formatting | bytes 153600
  43.1 1.1 %copy.17 = f32[16]{0:T(128)} copy(f32[16]{0:T(128)} %bitcast.14) | data formatting | bytes 128
  44.2 1.2 %copy.18 = f32[16]{0:T(128)} copy(f32[16]{0:T(128)} %bitcast.13) | data formatting | bytes 128

commit v2 on v1

--- a/solution.py
+++ b/solution.py
@@ -18,6 +18,7 @@
 SHIFT = PAIR - WINDOW
 LANES = 128
 BLOCK = 16
+PITCH_EXTRA = 4
 VMEM_LIMIT = 60 * 1024 * 1024
 F32 = jnp.float32
 MESH = pl.DeviceIdType.MESH
@@ -57,9 +58,8 @@
     fields_hbm,
     weight_ref,
     bias_ref,
-    energy_ref,
-    new_ref,
-    mixed_ref,
+    total_ref,
+    mean_ref,
     greens,
     fields,
     raw,
@@ -101,6 +101,7 @@
     per_vector = chol_hbm.shape[1]
     kpoints = greens.shape[0] // walkers
     tiles = per_vector // slots
+    pitch = wide.shape[0] // BLOCK
     pairs = OCCUPIED_COUNT // 2
     lines = devices // 2
     parity, line = lax.rem(me, 2), me // 2
@@ -168,10 +169,10 @@
     def split(block, carry):
         first = pl.multiple_of(block * BLOCK, BLOCK)
         for n in range(BLOCK):
-            wide[n * per_vector : (n + 1) * per_vector, :] = raw[first + n].astype(F32)
+            wide[n * pitch : n * pitch + per_vector, :] = raw[first + n].astype(F32)
         for slot in range(slots):
             for tile in range(tiles):
-                part = wide[pl.ds(tile * slots + slot, BLOCK, stride=per_vector), :]
+                part = wide[pl.ds(tile * slots + slot, BLOCK, stride=pitch), :]
                 chol[slot, pl.ds(first, BLOCK), tile * LANES : (tile + 1) * LANES] = part.astype(chol.dtype)
         return carry
 
@@ -352,8 +353,8 @@
         share_copy(step).wait_recv()
         real = real + landed[step - 1, 0]
         imag = imag + landed[step - 1, 1]
-    bias_ref[:, 0, :] = real
-    bias_ref[:, 1, :] = imag
+    bias_ref[0] = real
+    bias_ref[1] = imag
     coulomb = jnp.sum(real * real - imag * imag, axis=1, keepdims=True)
     mixed_part = jnp.sum(real * imag, axis=1, keepdims=True)
     square = SQRT_STEP * SQRT_STEP
@@ -386,6 +387,7 @@
     for index in range(devices):
         step = lax.rem(me + devices - index, devices)
         total = total + jnp.where(step == 0, packed, other_sums[jnp.maximum(step - 1, 0)])
+    total_ref[...] = total
     energy = total[:, 0:1]
     weighted = jnp.sum(weight * energy, axis=0, keepdims=True)
     weights = jnp.sum(weight, axis=0, keepdims=True)
@@ -393,15 +395,13 @@
     mean = jnp.where(lane == 0, weighted, jnp.where(lane == 1, weights, 0.0))
     own_mean[...] = mean
     means = send_all(own_mean, other_mean, mean_send, mean_recv, walk_peer, groups)
-    energy_ref[...] = row_from(energy)
-    new_ref[...] = row_from(weight * jnp.exp(total[:, 1:2]) * jnp.maximum(jnp.cos(total[:, 2:3]), 0.0))
     for copy in means:
         copy.wait_recv()
     total = jnp.zeros_like(mean)
     for index in range(groups):
         step = lax.rem(group + groups - index, groups)
         total = total + jnp.where(step == 0, mean, other_mean[jnp.maximum(step - 1, 0)])
-    mixed_ref[...] = total[0:1, 0:1] / total[0:1, 1:2]
+    mean_ref[...] = total
     for slot in range(1, slots):
         green_copy(slot).wait_send()
     for slot in range(slots):
@@ -410,6 +410,17 @@
         share_copy(step).wait_send()
     for copy in sums + means:
         copy.wait_send()
+
+
+def finish_kernel(sums_ref, total_ref, mean_ref, weight_ref, bias_ref, energy_ref, new_ref, mixed_ref):
+    bias_ref[:, 0, :] = sums_ref[0]
+    bias_ref[:, 1, :] = sums_ref[1]
+    total = total_ref[...]
+    weight = column_of(weight_ref[...])
+    energy_ref[...] = row_from(total[:, 0:1])
+    new_ref[...] = row_from(weight * jnp.exp(total[:, 1:2]) * jnp.maximum(jnp.cos(total[:, 2:3]), 0.0))
+    mean = mean_ref[:1, :]
+    mixed_ref[...] = mean[:, 0:1] / mean[:, 1:2]
 
 
 def local(greens, cholesky, slot_source, block_transfer_index, slot_multiplicity, fields, weight):
@@ -433,21 +444,20 @@
     by_vector = (
         cholesky.reshape(slots, vectors, tiles, LANES).transpose(1, 2, 0, 3).reshape(vectors, tiles * slots, LANES)
     )
-    bias, energy, new_weight, mixed = pl.pallas_call(
+    sums, total, mean = pl.pallas_call(
         functools.partial(step_kernel, devices, groups),
         out_shape=(
-            jax.ShapeDtypeStruct((walkers, 2, width), F32),
-            jax.ShapeDtypeStruct((1, walkers), F32),
-            jax.ShapeDtypeStruct((1, walkers), F32),
-            jax.ShapeDtypeStruct((1, 1), F32),
+            jax.ShapeDtypeStruct((2, walkers, width), F32),
+            jax.ShapeDtypeStruct((walkers, LANES), F32),
+            jax.ShapeDtypeStruct((8, LANES), F32),
         ),
         in_specs=[smem, smem, smem, hbm, hbm, hbm, vmem],
-        out_specs=(vmem,) * 4,
+        out_specs=(vmem,) * 3,
         scratch_shapes=[
             pltpu.VMEM((walkers * kpoints, flat), half),
             pltpu.VMEM(fields.shape, F32),
             pltpu.VMEM((padded, tiles * slots, LANES), half),
-            pltpu.VMEM((BLOCK * tiles * slots, LANES), F32),
+            pltpu.VMEM((BLOCK * (tiles * slots + PITCH_EXTRA), LANES), F32),
             pltpu.VMEM((slots, padded, flat), half),
             pltpu.VMEM((slots - 1, walkers, flat), half),
             pltpu.VMEM((slots, walkers, flat), half),
@@ -489,6 +499,18 @@
         fields,
         weight.reshape(1, walkers),
     )
+    bias, energy, new_weight, mixed = pl.pallas_call(
+        finish_kernel,
+        out_shape=(
+            jax.ShapeDtypeStruct((walkers, 2, width), F32),
+            jax.ShapeDtypeStruct((1, walkers), F32),
+            jax.ShapeDtypeStruct((1, walkers), F32),
+            jax.ShapeDtypeStruct((1, 1), F32),
+        ),
+        in_specs=[vmem] * 4,
+        out_specs=(vmem,) * 4,
+        name="finish",
+    )(sums, total, mean, weight.reshape(1, walkers))
     return bias, energy.reshape(walkers), new_weight.reshape(walkers), mixed.reshape(())
 
 

time: 47.3 us -> 36.9 us (0.78)
  Pallas kernels: 40.9 us -> 36.1 us
  local copies, waits for them, and re-layouts: 3.83 us -> 0 us
  between operations: 2.33 us -> 0.64 us
    pallas_call x1, Pallas kernels: 40.9 us -> 34.4 us  [local(): pl.pallas_call(functools.partial(step_kernel, devices, groups), out_shape...]
    unnamed x3 -> x0, local copies, waits for them, and re-layouts: 3.83 us -> none
    pallas_call x0 -> x1, Pallas kernels: none -> 1.7 us  [local(): pl.pallas_call(finish_kernel, out_shape=(jax.ShapeDtypeStruct((walkers, 2...]
where the time goes in v2:
time: 36.9 us; the launch traced here: 36.8 us
  Pallas kernels  36.1 us (98%)
  between operations  0.64 us (2%)
    pallas_call x1, Pallas kernels, local(): pl.pallas_call(functools.partial(step_kernel, devices, groups), out_shape...  34.4 us
    pallas_call x1, Pallas kernels, local(): pl.pallas_call(finish_kernel, out_shape=(jax.ShapeDtypeStruct((walkers, 2...  1.7 us

profile of v2, /device:TPU:0, one launch (start us, length us, event | category | flops | bytes accessed | tf_op | source)
XLA Modules:
  0.0 36.8 jit_solution(1620751004921120792)
XLA Ops:
  0.6 34.4 %step.1 = (f32[2,16,600]{2,1,0:T(8,128)}, f32[16,128]{1,0:T(8,128)}, f32[8,128]{1,0:T(8,128)}) custom-call(s32[32]{0:T(128)} %source_ref.1, s32[4]{0:T(128)} %transfer_ref.1, s32[4]{0:T(128)} %multiple_ref.1, bf16[128,3072]{1,0:T(8,128)(2,1)} %bitcast.11, bf16[300,96,128]{2,1,0:T(8,128)(2,1)} %bitcast.10, f32[16,16,300]{2,1,0:T(8,128)} %fields_hbm.1, ...), custom_call_target="tpu_custom_call" | custom-call | tf_op jit(solution)/shard_map/step/pallas_call | solution.py:447
  35.1 1.7 %finish.1 = (f32[16,2,600]{2,1,0:T(2,128)}, f32[1,16]{1,0:T(1,128)}, f32[1,16]{1,0:T(1,128)}, f32[1,1]{1,0:T(1,128)}) custom-call(f32[2,16,600]{2,1,0:T(8,128)} %get-tuple-element.11.sums_ref, f32[16,128]{1,0:T(8,128)} %get-tuple-element.12.total_ref, f32[8,128]{1,0:T(8,128)} %get-tuple-element.13.mean_ref, f32[1,16]{1,0:T(1,128)} %bitcast.13), custom_call_target="tpu_custom_call" | custom-call | tf_op jit(solution)/shard_map/finish/pallas_call | solution.py:502

commit v3 on v2

--- a/solution.py
+++ b/solution.py
@@ -40,11 +40,6 @@
 def column_of(row):
     count = row.shape[1]
     return jnp.sum(jnp.where(on_diagonal(count), jnp.broadcast_to(row, (count, count)), 0.0), axis=1, keepdims=True)
-
-
-def row_from(column):
-    count = column.shape[0]
-    return jnp.sum(jnp.where(on_diagonal(count), jnp.broadcast_to(column, (count, count)), 0.0), axis=0, keepdims=True)
 
 
 def step_kernel(
@@ -59,7 +54,6 @@
     weight_ref,
     bias_ref,
     total_ref,
-    mean_ref,
     greens,
     fields,
     raw,
@@ -78,10 +72,7 @@
     linear,
     summed,
     landed,
-    own_sums,
-    other_sums,
-    own_mean,
-    other_mean,
+    packets,
     local_sem,
     green_send,
     green_recv,
@@ -91,8 +82,6 @@
     share_recv,
     sum_send,
     sum_recv,
-    mean_send,
-    mean_recv,
 ):
     me = lax.axis_index("pb")
     group = lax.axis_index("walk")
@@ -111,14 +100,22 @@
     def pb_peer(step):
         return {"pb": lax.rem(me + step, devices)}
 
-    def walk_peer(step):
-        return {"walk": lax.rem(group + step, groups)}
+    everyone = devices * groups
+
+    def peer_of(step):
+        return {"walk": lax.rem(group + step // devices, groups), "pb": lax.rem(me + lax.rem(step, devices), devices)}
+
+    def sender_of(step):
+        walk = lax.rem(group + groups - step // devices, groups)
+        return walk * devices + lax.rem(me + devices - lax.rem(step, devices), devices)
 
     barrier = pltpu.get_barrier_semaphore()
-    for step in range(1, devices):
-        pl.semaphore_signal(barrier, inc=1, device_id=pb_peer(step), device_id_type=MESH)
-    for step in range(1, groups):
-        pl.semaphore_signal(barrier, inc=1, device_id=walk_peer(step), device_id_type=MESH)
+
+    def greet(step, carry):
+        pl.semaphore_signal(barrier, inc=1, device_id=peer_of(step), device_id_type=MESH)
+        return carry
+
+    lax.fori_loop(1, everyone, greet, 0)
 
     green_in = pltpu.make_async_copy(greens_hbm, greens, local_sem.at[0])
     green_in.start()
@@ -151,7 +148,7 @@
         for slot in range(1, slots):
             picked[slot - 1, :, first : first + span] = rows[slot * walkers : (slot + 1) * walkers]
 
-    pl.semaphore_wait(barrier, devices + groups - 2)
+    pl.semaphore_wait(barrier, everyone - 1)
 
     def green_copy(slot):
         return pltpu.make_async_remote_copy(
@@ -322,10 +319,15 @@
 
         @pl.when(slot == 1)
         def _():
-            for other in range(1, slots):
-                green_copy(other).wait_recv()
-
             def one(other, inner):
+                pltpu.make_async_remote_copy(
+                    src_ref=picked.at[other - 1],
+                    dst_ref=arrived.at[other],
+                    send_sem=green_send.at[other - 1],
+                    recv_sem=green_recv.at[other - 1],
+                    device_id={"pb": 2 * line + 1 - parity},
+                    device_id_type=MESH,
+                ).wait_recv()
                 traces(other)
                 return inner
 
@@ -361,66 +363,82 @@
     real_arg = SQRT_STEP * jnp.sum(linear[0], axis=1, keepdims=True) - (0.5 * square) * coulomb
     imag_arg = SQRT_STEP * jnp.sum(linear[1], axis=1, keepdims=True) - square * mixed_part
     energy_part = 0.5 * coulomb - 0.5 * jnp.sum(crossed[...], axis=1, keepdims=True)
-    lane = lax.broadcasted_iota(jnp.int32, own_sums.shape, 1)
-    packed = jnp.where(lane == 0, energy_part, jnp.where(lane == 1, real_arg, jnp.where(lane == 2, imag_arg, 0.0)))
-    own_sums[...] = packed
-
-    def send_all(source, target, send_sems, recv_sems, peer, count):
-        copies = []
-        for step in range(1, count):
-            copy = pltpu.make_async_remote_copy(
-                src_ref=source,
-                dst_ref=target.at[step - 1],
-                send_sem=send_sems.at[step - 1],
-                recv_sem=recv_sems.at[step - 1],
-                device_id=peer(step),
-                device_id_type=MESH,
-            )
-            copy.start()
-            copies.append(copy)
-        return copies
-
-    sums = send_all(own_sums, other_sums, sum_send, sum_recv, pb_peer, devices)
-    for copy in sums:
-        copy.wait_recv()
-    total = jnp.zeros_like(packed)
+    shape = (walkers, LANES)
+    lane = lax.broadcasted_iota(jnp.int32, shape, 1)
+    row = lax.broadcasted_iota(jnp.int32, shape, 0)
+    values = (energy_part, real_arg, imag_arg)
+    packet = jnp.zeros(shape, F32)
+    for number, value in enumerate(values):
+        packet = jnp.where(lane == row + number * walkers, value, packet)
+    tail = len(values) * walkers
+    packet = jnp.where(lane == tail, weight * energy_part, packet)
+    packet = jnp.where(lane == tail + 1, weight * (1.0 / devices), packet)
+    packets[group * devices + me] = jnp.sum(packet, axis=0, keepdims=True)
+
+    def packet_out(step):
+        mine_at = group * devices + me
+        return pltpu.make_async_remote_copy(
+            src_ref=packets.at[mine_at],
+            dst_ref=packets.at[mine_at],
+            send_sem=sum_send.at[step - 1],
+            recv_sem=sum_recv.at[step - 1],
+            device_id=peer_of(step),
+            device_id_type=MESH,
+        )
+
+    def packet_in(step):
+        at = sender_of(step)
+        return pltpu.make_async_remote_copy(
+            src_ref=packets.at[at],
+            dst_ref=packets.at[at],
+            send_sem=sum_send.at[step - 1],
+            recv_sem=sum_recv.at[step - 1],
+            device_id=peer_of(step),
+            device_id_type=MESH,
+        )
+
+    def send_packet(step, carry):
+        packet_out(everyone - step).start()
+        return carry
+
+    def take_packet(step, carry):
+        packet_in(step).wait_recv()
+        return carry
+
+    def packet_sent(step, carry):
+        packet_out(step).wait_send()
+        return carry
+
+    lax.fori_loop(1, everyone, send_packet, 0)
+    lax.fori_loop(1, everyone, take_packet, 0)
+    total = jnp.zeros((1, LANES), F32)
     for index in range(devices):
-        step = lax.rem(me + devices - index, devices)
-        total = total + jnp.where(step == 0, packed, other_sums[jnp.maximum(step - 1, 0)])
-    total_ref[...] = total
-    energy = total[:, 0:1]
-    weighted = jnp.sum(weight * energy, axis=0, keepdims=True)
-    weights = jnp.sum(weight, axis=0, keepdims=True)
-    lane = lax.broadcasted_iota(jnp.int32, own_mean.shape, 1)
-    mean = jnp.where(lane == 0, weighted, jnp.where(lane == 1, weights, 0.0))
-    own_mean[...] = mean
-    means = send_all(own_mean, other_mean, mean_send, mean_recv, walk_peer, groups)
-    for copy in means:
-        copy.wait_recv()
-    total = jnp.zeros_like(mean)
-    for index in range(groups):
-        step = lax.rem(group + groups - index, groups)
-        total = total + jnp.where(step == 0, mean, other_mean[jnp.maximum(step - 1, 0)])
-    mean_ref[...] = total
+        total = total + packets[group * devices + index]
+    whole = jnp.zeros((1, LANES), F32)
+    for index in range(everyone):
+        whole = whole + packets[index]
+    lane = lax.broadcasted_iota(jnp.int32, (1, LANES), 1)
+    total_ref[...] = jnp.where(lane < tail, total, whole)
+    lax.fori_loop(1, everyone, packet_sent, 0)
     for slot in range(1, slots):
         green_copy(slot).wait_send()
     for slot in range(slots):
         pair_copy(slot).wait_send()
     for step in range(1, lines):
         share_copy(step).wait_send()
-    for copy in sums + means:
-        copy.wait_send()
-
-
-def finish_kernel(sums_ref, total_ref, mean_ref, weight_ref, bias_ref, energy_ref, new_ref, mixed_ref):
+
+
+def finish_kernel(sums_ref, total_ref, weight_ref, bias_ref, energy_ref, new_ref, mixed_ref):
     bias_ref[:, 0, :] = sums_ref[0]
     bias_ref[:, 1, :] = sums_ref[1]
     total = total_ref[...]
-    weight = column_of(weight_ref[...])
-    energy_ref[...] = row_from(total[:, 0:1])
-    new_ref[...] = row_from(weight * jnp.exp(total[:, 1:2]) * jnp.maximum(jnp.cos(total[:, 2:3]), 0.0))
-    mean = mean_ref[:1, :]
-    mixed_ref[...] = mean[:, 0:1] / mean[:, 1:2]
+    weight = weight_ref[...]
+    walkers = weight.shape[1]
+    energy_ref[...] = total[:, :walkers]
+    real, imag = total[:, walkers : 2 * walkers], total[:, 2 * walkers : 3 * walkers]
+    new_ref[...] = weight * jnp.exp(real) * jnp.maximum(jnp.cos(imag), 0.0)
+    tail = 3 * walkers
+    mixed_ref[...] = total[:, tail : tail + 1] / total[:, tail + 1 : tail + 2]
 
 
 def local(greens, cholesky, slot_source, block_transfer_index, slot_multiplicity, fields, weight):
@@ -444,15 +462,14 @@
     by_vector = (
         cholesky.reshape(slots, vectors, tiles, LANES).transpose(1, 2, 0, 3).reshape(vectors, tiles * slots, LANES)
     )
-    sums, total, mean = pl.pallas_call(
+    sums, total = pl.pallas_call(
         functools.partial(step_kernel, devices, groups),
         out_shape=(
             jax.ShapeDtypeStruct((2, walkers, width), F32),
-            jax.ShapeDtypeStruct((walkers, LANES), F32),
-            jax.ShapeDtypeStruct((8, LANES), F32),
+            jax.ShapeDtypeStruct((1, LANES), F32),
         ),
         in_specs=[smem, smem, smem, hbm, hbm, hbm, vmem],
-        out_specs=(vmem,) * 3,
+        out_specs=(vmem,) * 2,
         scratch_shapes=[
             pltpu.VMEM((walkers * kpoints, flat), half),
             pltpu.VMEM(fields.shape, F32),
@@ -472,10 +489,7 @@
             pltpu.VMEM((2, walkers, vectors), F32),
             pltpu.VMEM((lines, 2, walkers, width), F32),
             pltpu.VMEM((lines - 1, 2, walkers, width), F32),
-            pltpu.VMEM((walkers, LANES), F32),
-            pltpu.VMEM((devices - 1, walkers, LANES), F32),
-            pltpu.VMEM((8, LANES), F32),
-            pltpu.VMEM((max(groups - 1, 1), 8, LANES), F32),
+            pltpu.VMEM((devices * groups, 1, LANES), F32),
             dma((8,)),
             dma((slots - 1,)),
             dma((slots - 1,)),
@@ -483,10 +497,8 @@
             dma((slots,)),
             dma((lines - 1,)),
             dma((lines - 1,)),
-            dma((devices - 1,)),
-            dma((devices - 1,)),
-            dma((max(groups - 1, 1),)),
-            dma((max(groups - 1, 1),)),
+            dma((devices * groups - 1,)),
+            dma((devices * groups - 1,)),
         ],
         compiler_params=pltpu.CompilerParams(collective_id=1, has_side_effects=True, vmem_limit_bytes=VMEM_LIMIT),
         name="step",
@@ -507,10 +519,10 @@
             jax.ShapeDtypeStruct((1, walkers), F32),
             jax.ShapeDtypeStruct((1, 1), F32),
         ),
-        in_specs=[vmem] * 4,
+        in_specs=[vmem] * 3,
         out_specs=(vmem,) * 4,
         name="finish",
-    )(sums, total, mean, weight.reshape(1, walkers))
+    )(sums, total, weight.reshape(1, walkers))
     return bias, energy.reshape(walkers), new_weight.reshape(walkers), mixed.reshape(())
 
 

time: 36.9 us -> 36.2 us (0.981)
  Pallas kernels: 36.1 us -> 35.4 us
    pallas_call x1, Pallas kernels: 34.4 us -> 33.8 us  [local(): pl.pallas_call(functools.partial(step_kernel, devices, groups), out_shape...]
where the time goes in v3:
time: 36.2 us; the launch traced here: 36.1 us
  Pallas kernels  35.4 us (98%)
  between operations  0.64 us (2%)
    pallas_call x1, Pallas kernels, local(): pl.pallas_call(functools.partial(step_kernel, devices, groups), out_shape...  33.8 us
    pallas_call x1, Pallas kernels, local(): pl.pallas_call(finish_kernel, out_shape=(jax.ShapeDtypeStruct((walkers, 2...  1.62 us

profile of v3, /device:TPU:0, one launch (start us, length us, event | category | flops | bytes accessed | tf_op | source)
XLA Modules:
  0.0 36.1 jit_solution(15967119323090142731)
XLA Ops:
  0.6 33.8 %step.1 = (f32[2,16,600]{2,1,0:T(8,128)}, f32[1,128]{1,0:T(1,128)}) custom-call(s32[32]{0:T(128)} %source_ref.1, s32[4]{0:T(128)} %transfer_ref.1, s32[4]{0:T(128)} %multiple_ref.1, bf16[128,3072]{1,0:T(8,128)(2,1)} %bitcast.11, bf16[300,96,128]{2,1,0:T(8,128)(2,1)} %bitcast.10, f32[16,16,300]{2,1,0:T(8,128)} %fields_hbm.1, f32[1,16]{1,0:T(1,128)} %bitcast.12), custom_call_target="tpu_custom_call" | custom-call | tf_op jit(solution)/shard_map/step/pallas_call | solution.py:465
  34.5 1.6 %finish.1 = (f32[16,2,600]{2,1,0:T(2,128)}, f32[1,16]{1,0:T(1,128)}, f32[1,16]{1,0:T(1,128)}, f32[1,1]{1,0:T(1,128)}) custom-call(f32[2,16,600]{2,1,0:T(8,128)} %get-tuple-element.10.sums_ref, f32[1,128]{1,0:T(1,128)} %get-tuple-element.11.total_ref, f32[1,16]{1,0:T(1,128)} %bitcast.13), custom_call_target="tpu_custom_call" | custom-call | tf_op jit(solution)/shard_map/finish/pallas_call | solution.py:514

commit v4 on v3

--- a/solution.py
+++ b/solution.py
@@ -73,6 +73,7 @@
     summed,
     landed,
     packets,
+    means,
     local_sem,
     green_send,
     green_recv,
@@ -82,6 +83,8 @@
     share_recv,
     sum_send,
     sum_recv,
+    mean_send,
+    mean_recv,
 ):
     me = lax.axis_index("pb")
     group = lax.axis_index("walk")
@@ -100,22 +103,14 @@
     def pb_peer(step):
         return {"pb": lax.rem(me + step, devices)}
 
-    everyone = devices * groups
-
-    def peer_of(step):
-        return {"walk": lax.rem(group + step // devices, groups), "pb": lax.rem(me + lax.rem(step, devices), devices)}
-
-    def sender_of(step):
-        walk = lax.rem(group + groups - step // devices, groups)
-        return walk * devices + lax.rem(me + devices - lax.rem(step, devices), devices)
+    def walk_peer(step):
+        return {"walk": lax.rem(group + step, groups)}
 
     barrier = pltpu.get_barrier_semaphore()
-
-    def greet(step, carry):
-        pl.semaphore_signal(barrier, inc=1, device_id=peer_of(step), device_id_type=MESH)
-        return carry
-
-    lax.fori_loop(1, everyone, greet, 0)
+    for step in range(1, devices):
+        pl.semaphore_signal(barrier, inc=1, device_id=pb_peer(step), device_id_type=MESH)
+    for step in range(1, groups):
+        pl.semaphore_signal(barrier, inc=1, device_id=walk_peer(step), device_id_type=MESH)
 
     green_in = pltpu.make_async_copy(greens_hbm, greens, local_sem.at[0])
     green_in.start()
@@ -148,7 +143,7 @@
         for slot in range(1, slots):
             picked[slot - 1, :, first : first + span] = rows[slot * walkers : (slot + 1) * walkers]
 
-    pl.semaphore_wait(barrier, everyone - 1)
+    pl.semaphore_wait(barrier, devices + groups - 2)
 
     def green_copy(slot):
         return pltpu.make_async_remote_copy(
@@ -373,53 +368,50 @@
     tail = len(values) * walkers
     packet = jnp.where(lane == tail, weight * energy_part, packet)
     packet = jnp.where(lane == tail + 1, weight * (1.0 / devices), packet)
-    packets[group * devices + me] = jnp.sum(packet, axis=0, keepdims=True)
-
-    def packet_out(step):
-        mine_at = group * devices + me
-        return pltpu.make_async_remote_copy(
-            src_ref=packets.at[mine_at],
-            dst_ref=packets.at[mine_at],
-            send_sem=sum_send.at[step - 1],
-            recv_sem=sum_recv.at[step - 1],
-            device_id=peer_of(step),
-            device_id_type=MESH,
-        )
-
-    def packet_in(step):
-        at = sender_of(step)
-        return pltpu.make_async_remote_copy(
-            src_ref=packets.at[at],
-            dst_ref=packets.at[at],
-            send_sem=sum_send.at[step - 1],
-            recv_sem=sum_recv.at[step - 1],
-            device_id=peer_of(step),
-            device_id_type=MESH,
-        )
-
-    def send_packet(step, carry):
-        packet_out(everyone - step).start()
-        return carry
-
-    def take_packet(step, carry):
-        packet_in(step).wait_recv()
-        return carry
-
-    def packet_sent(step, carry):
-        packet_out(step).wait_send()
-        return carry
-
-    lax.fori_loop(1, everyone, send_packet, 0)
-    lax.fori_loop(1, everyone, take_packet, 0)
-    total = jnp.zeros((1, LANES), F32)
-    for index in range(devices):
-        total = total + packets[group * devices + index]
-    whole = jnp.zeros((1, LANES), F32)
-    for index in range(everyone):
-        whole = whole + packets[index]
+    packets[me] = jnp.sum(packet, axis=0, keepdims=True)
+
+    def send_all(held, at, count, send_sems, recv_sems, peer):
+        started = []
+        for step in range(1, count):
+            copy = pltpu.make_async_remote_copy(
+                src_ref=held.at[at],
+                dst_ref=held.at[at],
+                send_sem=send_sems.at[step - 1],
+                recv_sem=recv_sems.at[step - 1],
+                device_id=peer(step),
+                device_id_type=MESH,
+            )
+            copy.start()
+            started.append(copy)
+        return started
+
+    def take_all(held, at, count, send_sems, recv_sems, peer):
+        for step in range(1, count):
+            sender = lax.rem(at + count - step, count)
+            pltpu.make_async_remote_copy(
+                src_ref=held.at[sender],
+                dst_ref=held.at[sender],
+                send_sem=send_sems.at[step - 1],
+                recv_sem=recv_sems.at[step - 1],
+                device_id=peer(step),
+                device_id_type=MESH,
+            ).wait_recv()
+
+    sums = send_all(packets, me, devices, sum_send, sum_recv, pb_peer)
+    take_all(packets, me, devices, sum_send, sum_recv, pb_peer)
+    total = packets[0]
+    for index in range(1, devices):
+        total = total + packets[index]
+    means[group] = total
+    sums += send_all(means, group, groups, mean_send, mean_recv, walk_peer)
+    take_all(means, group, groups, mean_send, mean_recv, walk_peer)
+    whole = means[0]
+    for index in range(1, groups):
+        whole = whole + means[index]
     lane = lax.broadcasted_iota(jnp.int32, (1, LANES), 1)
     total_ref[...] = jnp.where(lane < tail, total, whole)
-    lax.fori_loop(1, everyone, packet_sent, 0)
+    for copy in sums:
+        copy.wait_send()
     for slot in range(1, slots):
         green_copy(slot).wait_send()
     for slot in range(slots):
@@ -489,7 +481,8 @@
             pltpu.VMEM((2, walkers, vectors), F32),
             pltpu.VMEM((lines, 2, walkers, width), F32),
             pltpu.VMEM((lines - 1, 2, walkers, width), F32),
-            pltpu.VMEM((devices * groups, 1, LANES), F32),
+            pltpu.VMEM((devices, 1, LANES), F32),
+            pltpu.VMEM((groups, 1, LANES), F32),
             dma((8,)),
             dma((slots - 1,)),
             dma((slots - 1,)),
@@ -497,8 +490,10 @@
             dma((slots,)),
             dma((lines - 1,)),
             dma((lines - 1,)),
-            dma((devices * groups - 1,)),
-            dma((devices * groups - 1,)),
+            dma((devices - 1,)),
+            dma((devices - 1,)),
+            dma((max(groups - 1, 1),)),
+            dma((max(groups - 1, 1),)),
         ],
         compiler_params=pltpu.CompilerParams(collective_id=1, has_side_effects=True, vmem_limit_bytes=VMEM_LIMIT),
         name="step",

time: 36.2 us -> 36 us (level)
  no operation moved by 1% of the time
where the time goes in v4:
time: 36 us; the launch traced here: 35.8 us
  Pallas kernels  35.2 us (98%)
  between operations  0.64 us (2%)
    pallas_call x1, Pallas kernels, local(): pl.pallas_call(functools.partial(step_kernel, devices, groups), out_shape...  33.6 us
    pallas_call x1, Pallas kernels, local(): pl.pallas_call(finish_kernel, out_shape=(jax.ShapeDtypeStruct((walkers, 2...  1.62 us

profile of v4, /device:TPU:0, one launch (start us, length us, event | category | flops | bytes accessed | tf_op | source)
XLA Modules:
  0.0 35.8 jit_solution(7174640775999708922)
XLA Ops:
  0.6 33.6 %step.1 = (f32[2,16,600]{2,1,0:T(8,128)}, f32[1,128]{1,0:T(1,128)}) custom-call(s32[32]{0:T(128)} %source_ref.1, s32[4]{0:T(128)} %transfer_ref.1, s32[4]{0:T(128)} %multiple_ref.1, bf16[128,3072]{1,0:T(8,128)(2,1)} %bitcast.11, bf16[300,96,128]{2,1,0:T(8,128)(2,1)} %bitcast.10, f32[16,16,300]{2,1,0:T(8,128)} %fields_hbm.1, f32[1,16]{1,0:T(1,128)} %bitcast.12), custom_call_target="tpu_custom_call" | custom-call | tf_op jit(solution)/shard_map/step/pallas_call | solution.py:457
  34.2 1.6 %finish.1 = (f32[16,2,600]{2,1,0:T(2,128)}, f32[1,16]{1,0:T(1,128)}, f32[1,16]{1,0:T(1,128)}, f32[1,1]{1,0:T(1,128)}) custom-call(f32[2,16,600]{2,1,0:T(8,128)} %get-tuple-element.10.sums_ref, f32[1,128]{1,0:T(1,128)} %get-tuple-element.11.total_ref, f32[1,16]{1,0:T(1,128)} %bitcast.13), custom_call_target="tpu_custom_call" | custom-call | tf_op jit(solution)/shard_map/finish/pallas_call | solution.py:509

commit v5 on v4

--- a/solution.py
+++ b/solution.py
@@ -72,6 +72,7 @@
     linear,
     summed,
     landed,
+    relay,
     packets,
     means,
     local_sem,
@@ -81,6 +82,7 @@
     pair_recv,
     share_send,
     share_recv,
+    relay_recv,
     sum_send,
     sum_recv,
     mean_send,
@@ -106,6 +108,7 @@
     def walk_peer(step):
         return {"walk": lax.rem(group + step, groups)}
 
+    landed[...] = jnp.zeros_like(landed)
     barrier = pltpu.get_barrier_semaphore()
     for step in range(1, devices):
         pl.semaphore_signal(barrier, inc=1, device_id=pb_peer(step), device_id_type=MESH)
@@ -280,6 +283,56 @@
             device_id_type=MESH,
         )
 
+    last_line = lines - 1
+
+    def relay_copy(step):
+        return pltpu.make_async_remote_copy(
+            src_ref=summed.at[step],
+            dst_ref=relay,
+            send_sem=share_send.at[step - 1],
+            recv_sem=relay_recv.at[0],
+            device_id={"pb": 2 * jnp.where(line == 0, 1, lines - 2) + parity},
+            device_id_type=MESH,
+        )
+
+    def handed_on(step):
+        if lines < 4 or step not in (1, last_line):
+            return None
+        return line == (0 if step == last_line else last_line)
+
+    def handed_to_me(step):
+        if lines < 4 or step not in (2, lines - 2):
+            return None
+        if lines == 4:
+            return (line == 1) | (line == 2)
+        return line == (1 if step == lines - 2 else lines - 2)
+
+    def not_sent_here(step):
+        if lines < 4 or step not in (1, last_line):
+            return None
+        return line == (last_line if step == last_line else 0)
+
+    def either(condition, yes, no):
+        if condition is None:
+            no()
+            return
+
+        @pl.when(condition)
+        def _():
+            yes()
+
+        @pl.when(jnp.logical_not(condition))
+        def _():
+            no()
+
+    def nothing():
+        pass
+
+    def forward(step):
+        relay_copy(step).wait_recv()
+        summed[step] += relay[...]
+        share_copy(step).start()
+
     def terms_of(transfer, part):
         value = jnp.zeros((walkers, vectors), F32)
         for held in (mine, theirs):
@@ -305,7 +358,8 @@
                     taken = jnp.where(piece == index, value[:, index * width : (index + 1) * width], taken)
                 summed[step, part] = taken
 
-    order = [lines // 2] + [step for step in range(1, lines) if step != lines // 2]
+    first_sent = [step for step in (last_line, 1) if step < lines]
+    order = list(dict.fromkeys(first_sent + [lines // 2] + list(range(1, lines))))
 
     def round_of(slot, carry):
         @pl.when(slot == 0)
@@ -336,18 +390,24 @@
                 pair_copy(held).wait_recv()
             for step in order:
                 share_of(step)
-                share_copy(step).start()
+                if handed_on(step) is not None:
+                    either(handed_on(step), lambda: relay_copy(step).start(), lambda: share_copy(step).start())
+                else:
+                    either(handed_to_me(step), nothing, lambda: share_copy(step).start())
             share_of(0)
 
         return carry
 
     lax.fori_loop(0, slots, round_of, 0)
 
+    for step in range(1, lines):
+        if handed_to_me(step) is not None:
+            either(handed_to_me(step), lambda: forward(step), nothing)
     weight = column_of(weight_ref[...])
     real = summed[0, 0]
     imag = summed[0, 1]
     for step in range(1, lines):
-        share_copy(step).wait_recv()
+        either(not_sent_here(step), nothing, lambda: share_copy(step).wait_recv())
         real = real + landed[step - 1, 0]
         imag = imag + landed[step - 1, 1]
     bias_ref[0] = real
@@ -417,7 +477,7 @@
     for slot in range(slots):
         pair_copy(slot).wait_send()
     for step in range(1, lines):
-        share_copy(step).wait_send()
+        either(handed_on(step), lambda: relay_copy(step).wait_send(), lambda: share_copy(step).wait_send())
 
 
 def finish_kernel(sums_ref, total_ref, weight_ref, bias_ref, energy_ref, new_ref, mixed_ref):
@@ -481,6 +541,7 @@
             pltpu.VMEM((2, walkers, vectors), F32),
             pltpu.VMEM((lines, 2, walkers, width), F32),
             pltpu.VMEM((lines - 1, 2, walkers, width), F32),
+            pltpu.VMEM((2, walkers, width), F32),
             pltpu.VMEM((devices, 1, LANES), F32),
             pltpu.VMEM((groups, 1, LANES), F32),
             dma((8,)),
@@ -490,6 +551,7 @@
             dma((slots,)),
             dma((lines - 1,)),
             dma((lines - 1,)),
+            dma((1,)),
             dma((devices - 1,)),
             dma((devices - 1,)),
             dma((max(groups - 1, 1),)),

time: 36 us -> 36.9 us (1.025)
  Pallas kernels: 35.2 us -> 36.1 us
    pallas_call x1, Pallas kernels: 33.6 us -> 34.4 us  [local(): pl.pallas_call(functools.partial(step_kernel, devices, groups), out_shape...]
where the time goes in v5:
time: 36.9 us; the launch traced here: 36.7 us
  Pallas kernels  36.1 us (98%)
  between operations  0.64 us (2%)
    pallas_call x1, Pallas kernels, local(): pl.pallas_call(functools.partial(step_kernel, devices, groups), out_shape...  34.4 us
    pallas_call x1, Pallas kernels, local(): pl.pallas_call(finish_kernel, out_shape=(jax.ShapeDtypeStruct((walkers, 2...  1.62 us

profile of v5, /device:TPU:0, one launch (start us, length us, event | category | flops | bytes accessed | tf_op | source)
XLA Modules:
  0.0 36.7 jit_solution(9768127569614894828)
XLA Ops:
  0.6 34.4 %step.1 = (f32[2,16,600]{2,1,0:T(8,128)}, f32[1,128]{1,0:T(1,128)}) custom-call(s32[32]{0:T(128)} %source_ref.1, s32[4]{0:T(128)} %transfer_ref.1, s32[4]{0:T(128)} %multiple_ref.1, bf16[128,3072]{1,0:T(8,128)(2,1)} %bitcast.11, bf16[300,96,128]{2,1,0:T(8,128)(2,1)} %bitcast.10, f32[16,16,300]{2,1,0:T(8,128)} %fields_hbm.1, f32[1,16]{1,0:T(1,128)} %bitcast.12), custom_call_target="tpu_custom_call" | custom-call | tf_op jit(solution)/shard_map/step/pallas_call | solution.py:517
  35.1 1.6 %finish.1 = (f32[16,2,600]{2,1,0:T(2,128)}, f32[1,16]{1,0:T(1,128)}, f32[1,16]{1,0:T(1,128)}, f32[1,1]{1,0:T(1,128)}) custom-call(f32[2,16,600]{2,1,0:T(8,128)} %get-tuple-element.10.sums_ref, f32[1,128]{1,0:T(1,128)} %get-tuple-element.11.total_ref, f32[1,16]{1,0:T(1,128)} %bitcast.13), custom_call_target="tpu_custom_call" | custom-call | tf_op jit(solution)/shard_map/finish/pallas_call | solution.py:571

commit v6 on v4

--- a/solution.py
+++ b/solution.py
@@ -344,20 +344,24 @@
     lax.fori_loop(0, slots, round_of, 0)
 
     weight = column_of(weight_ref[...])
+    linear_real = SQRT_STEP * jnp.sum(linear[0], axis=1, keepdims=True)
+    linear_imag = SQRT_STEP * jnp.sum(linear[1], axis=1, keepdims=True)
+    half_cross = 0.5 * jnp.sum(crossed[...], axis=1, keepdims=True)
     real = summed[0, 0]
     imag = summed[0, 1]
     for step in range(1, lines):
         share_copy(step).wait_recv()
         real = real + landed[step - 1, 0]
         imag = imag + landed[step - 1, 1]
-    bias_ref[0] = real
-    bias_ref[1] = imag
+    summed[0, 0] = real
+    summed[0, 1] = imag
+    bias_out = pltpu.make_async_copy(summed.at[0], bias_ref, local_sem.at[7])
     coulomb = jnp.sum(real * real - imag * imag, axis=1, keepdims=True)
     mixed_part = jnp.sum(real * imag, axis=1, keepdims=True)
     square = SQRT_STEP * SQRT_STEP
-    real_arg = SQRT_STEP * jnp.sum(linear[0], axis=1, keepdims=True) - (0.5 * square) * coulomb
-    imag_arg = SQRT_STEP * jnp.sum(linear[1], axis=1, keepdims=True) - square * mixed_part
-    energy_part = 0.5 * coulomb - 0.5 * jnp.sum(crossed[...], axis=1, keepdims=True)
+    real_arg = linear_real - (0.5 * square) * coulomb
+    imag_arg = linear_imag - square * mixed_part
+    energy_part = 0.5 * coulomb - half_cross
     shape = (walkers, LANES)
     lane = lax.broadcasted_iota(jnp.int32, shape, 1)
     row = lax.broadcasted_iota(jnp.int32, shape, 0)
@@ -397,6 +401,7 @@
                 device_id_type=MESH,
             ).wait_recv()
 
+    bias_out.start()
     sums = send_all(packets, me, devices, sum_send, sum_recv, pb_peer)
     take_all(packets, me, devices, sum_send, sum_recv, pb_peer)
     total = packets[0]
@@ -410,6 +415,7 @@
         whole = whole + means[index]
     lane = lax.broadcasted_iota(jnp.int32, (1, LANES), 1)
     total_ref[...] = jnp.where(lane < tail, total, whole)
+    bias_out.wait()
     for copy in sums:
         copy.wait_send()
     for slot in range(1, slots):
@@ -461,7 +467,7 @@
             jax.ShapeDtypeStruct((1, LANES), F32),
         ),
         in_specs=[smem, smem, smem, hbm, hbm, hbm, vmem],
-        out_specs=(vmem,) * 2,
+        out_specs=(hbm, vmem),
         scratch_shapes=[
             pltpu.VMEM((walkers * kpoints, flat), half),
             pltpu.VMEM(fields.shape, F32),

time: 36 us -> 36 us (level)
  no operation moved by 1% of the time
where the time goes in v6:
time: 36 us; the launch traced here: 35.8 us
  Pallas kernels  35.2 us (98%)
  between operations  0.64 us (2%)
    pallas_call x1, Pallas kernels, local(): pl.pallas_call(functools.partial(step_kernel, devices, groups), out_shape...  33.5 us
    pallas_call x1, Pallas kernels, local(): pl.pallas_call(finish_kernel, out_shape=(jax.ShapeDtypeStruct((walkers, 2...  1.62 us

profile of v6, /device:TPU:0, one launch (start us, length us, event | category | flops | bytes accessed | tf_op | source)
XLA Modules:
  0.0 35.8 jit_solution(1433502812426276846)
XLA Ops:
  0.6 33.5 %step.1 = (f32[2,16,600]{2,1,0:T(8,128)}, f32[1,128]{1,0:T(1,128)}) custom-call(s32[32]{0:T(128)} %source_ref.1, s32[4]{0:T(128)} %transfer_ref.1, s32[4]{0:T(128)} %multiple_ref.1, bf16[128,3072]{1,0:T(8,128)(2,1)} %bitcast.11, bf16[300,96,128]{2,1,0:T(8,128)(2,1)} %bitcast.10, f32[16,16,300]{2,1,0:T(8,128)} %fields_hbm.1, f32[1,16]{1,0:T(1,128)} %bitcast.12), custom_call_target="tpu_custom_call" | custom-call | tf_op jit(solution)/shard_map/step/pallas_call | solution.py:463
  34.2 1.6 %finish.1 = (f32[16,2,600]{2,1,0:T(2,128)}, f32[1,16]{1,0:T(1,128)}, f32[1,16]{1,0:T(1,128)}, f32[1,1]{1,0:T(1,128)}) custom-call(f32[2,16,600]{2,1,0:T(8,128)} %get-tuple-element.10.sums_ref, f32[1,128]{1,0:T(1,128)} %get-tuple-element.11.total_ref, f32[1,16]{1,0:T(1,128)} %bitcast.13), custom_call_target="tpu_custom_call" | custom-call | tf_op jit(solution)/shard_map/finish/pallas_call | solution.py:515
